TPU v7x, 256 devices: a whole 4x4x8 slice. The times are simulated.
256 devices in a mesh: space: 64 (over z, y, core), tm: 4 (over x).
Axes of the slice: x: 4, y: 4, z: 8, core: 2. Of those that a mesh axis runs over, the one named last changes fastest.
Arguments:
- snapshots: bfloat16 [256, 524288], P('tm', 'space'), may hold values from -75 to 75
- prior_basis: bfloat16 [256, 524288], P('tm', 'space'), may hold values from -75 to 75
- mass_factor: bfloat16 [7, 64, 524288], P(None, None, 'space'), may hold values from -1 to 3.2, as said below
- neighbours: int32 [8192, 7], P('space'), may hold values from 0 to 8191, as said below
Outputs:
- merged_basis: bfloat16 [64, 524288], P(None, ('space', 'tm'))
- merged_weighted: bfloat16 [64, 524288], P(None, ('space', 'tm'))
Inputs may be any that keep to these rules, and one draw needn't show every extreme that they name: `mass_factor`: factor entries; the diagonal of each block's own coupling lies in 1.5 to 3. neighbours[i, 0] = i; every entry lies within 8 blocks of i; in every draw some entries lie exactly 8 blocks below and above their block.
All inputs are finite; a program needn't handle non-finite values.
Results may differ from a plain program's by a relative error of at most 0.018.
Values may be sent and summed in bfloat16 or wider, within the bound.
A program may use at most 128 MiB of HBM per device.

v0:
```python
import jax
import jax.numpy as jnp
from jax import lax
from jax.sharding import PartitionSpec as P

BLOCK_DOFS = 64
RANK = 64
NEIGHBOURS = 7
REACH = 8
SUBSPACE_STEPS = 3
LOCAL_BLOCKS = 128


def padded(block, sides, width):
    for axis, dim in sides:
        count = lax.axis_size(axis)
        forward = [(i, i + 1) for i in range(count - 1)]
        backward = [(target, source) for source, target in forward]
        low = lax.ppermute(
            lax.slice_in_dim(block, block.shape[dim] - width, None, axis=dim), axis, forward
        )
        high = lax.ppermute(lax.slice_in_dim(block, 0, width, axis=dim), axis, backward)
        block = jnp.concatenate([low, block, high], axis=dim)
    return block


def partner(block, axis, bit):
    count = lax.axis_size(axis)
    route = []
    for low in range(count):
        high = low | 1 << bit
        if high != low and high < count:
            route += [(low, high), (high, low)]
    return lax.ppermute(block, axis, route)


def weigh_rows(stacked, mass_factor, local_index):
    columns = stacked.shape[0]
    widened = padded(stacked, (("space", 1),), REACH * BLOCK_DOFS)
    blocks = widened.reshape(columns, -1, BLOCK_DOFS)
    picked = jnp.take(blocks, local_index, axis=1)
    factor = mass_factor.reshape(NEIGHBOURS, BLOCK_DOFS, -1, BLOCK_DOFS)
    result = jnp.einsum("cbkq,kqbr->cbr", picked, factor, preferred_element_type=jnp.float32)
    return result.reshape(columns, -1).astype(jnp.bfloat16)


def compress(gram_total):
    highest = lax.Precision.HIGHEST
    order_size = gram_total.shape[0]
    weights = jnp.eye(order_size, RANK, dtype=jnp.float32)
    for repeat in range(SUBSPACE_STEPS):
        product = jnp.dot(gram_total, weights, precision=highest)
        inner_gram = jnp.dot(
            product.T, jnp.dot(gram_total, product, precision=highest), precision=highest
        )
        scales = jnp.sqrt(jnp.diagonal(inner_gram))
        factor_lower = jnp.linalg.cholesky(inner_gram / (scales[:, None] * scales[None, :]))
        normed = product / scales[None, :]
        weights = lax.linalg.triangular_solve(
            factor_lower, normed, left_side=False, lower=True, transpose_a=True
        )
    product = jnp.dot(gram_total, weights, precision=highest)
    lengths = jnp.sqrt(jnp.sum(product * product, axis=0) + 1e-06)
    return (weights * lengths[None, :]).astype(jnp.bfloat16)


def coefficients_of(weighted):
    local_gram = jnp.dot(weighted, weighted.T, preferred_element_type=jnp.float32)
    return compress(lax.psum(local_gram, "space"))


def apply_coefficients(coefficients, stacked, weighted):
    basis = jnp.dot(coefficients.T, stacked, preferred_element_type=jnp.float32).astype(
        jnp.bfloat16
    )
    weighted_basis = jnp.dot(coefficients.T, weighted, preferred_element_type=jnp.float32).astype(
        jnp.bfloat16
    )
    return (basis, weighted_basis)


def ordered(upper_half, own_rows, partner_rows):
    lower_part = jnp.where(upper_half, partner_rows, own_rows)
    upper_part = jnp.where(upper_half, own_rows, partner_rows)
    return jnp.concatenate([lower_part, upper_part], axis=0)


def shards(snapshots, prior_basis, mass_factor, neighbours):
    local_index = neighbours - (lax.axis_index("space") * LOCAL_BLOCKS - REACH)
    stacked = jnp.concatenate([prior_basis, snapshots], axis=0)
    weighted = weigh_rows(stacked, mass_factor, local_index)
    basis, weighted_basis = apply_coefficients(coefficients_of(weighted), stacked, weighted)
    member = lax.axis_index("tm")
    for level_bit in range(lax.axis_size("tm").bit_length() - 1):
        upper_half = member // (1 << level_bit) % 2 == 1
        partner_weighted = partner(weighted_basis, "tm", level_bit)
        weighted = ordered(upper_half, weighted_basis, partner_weighted)
        coefficients = coefficients_of(weighted)
        partner_rows = partner(basis, "tm", level_bit)
        stacked = ordered(upper_half, basis, partner_rows)
        basis, weighted_basis = apply_coefficients(coefficients, stacked, weighted)
    share_width = basis.shape[1] // lax.axis_size("tm")
    basis_share = lax.dynamic_slice_in_dim(basis, member * share_width, share_width, 1)
    weighted_share = lax.dynamic_slice_in_dim(weighted_basis, member * share_width, share_width, 1)
    return (basis_share, weighted_share)


def solution(mesh):
    return jax.shard_map(
        shards,
        mesh=mesh,
        in_specs=(P("tm", "space"), P("tm", "space"), P(None, None, "space"), P("space", None)),
        out_specs=(P(None, ("space", "tm")), P(None, ("space", "tm"))),
        check_vma=False,
    )
```

profile of v0, /device:TPU:1, one launch (start us, length us, event | category | flops | bytes accessed | tf_op | source)
XLA Modules:
  0.0 817.4 jit_solution(14722766213442780236)
XLA Ops:
  19.5 20.9 %reshape.97 = bf16[7,64,128,64]{3,2,1,0:T(8,128)(2,1)} reshape(bf16[7,64,8192]{2,1,0:T(8,128)(2,1)} %param.9) | data formatting | bytes 14680064 | tf_op jit(solution)/shard_map/reshape | solution.py:42
  40.5 6.7 pad_maximum_fusion
  47.1 22.8 %gather_fusion = bf16[896,128,64]{1,2,0:T(8,128)(2,1)} fusion(bf16[128,144,64]{0,2,1:T(8,128)(2,1)S(1)} %bitcast.178, s32[1024]{0:T(1024)S(1)} %pad_clamp_fusion), kind=kCustom, calls=%fused_computation | custom fusion | bytes 29363712 | tf_op jit(solution)/shard_map/jit(_take)/gather | solution.py:41
  69.9 29.0 %bitcast_convert_fusion = bf16[128,128,64]{1,2,0:T(8,128)(2,1)S(1)} fusion(bf16[128,7,128,64]{2,3,1,0:T(8,128)(2,1)} %bitcast.179, pred[128,7]{1,0:T(8,128)(4,1)S(1)} %copy.29, bf16[7,64,128,64]{3,2,1,0:T(8,128)(2,1)} %reshape.97), kind=kOutput, calls=%fused_computation.20 | convolution fusion | flops 947912704 | bytes 24118144 | tf_op jit(solution)/shard_map/cbkq,kqbr->cbr/dot_general | solution.py:43
  100.4 174.6 %all-reduce.4.cloned.1.call-done = f32[128,128]{1,0:T(8,128)} async-done(((f32[128,128]{1,0:T(8,128)}), f32[128,128]{1,0:T(8,128)}) %all-reduce.4.cloned.1.call-update) | async-done | bytes 65552 | tf_op jit(solution)/shard_map/psum | solution.py:69
  278.5 5.8 cholesky.149
  285.7 4.9 custom-call.31
  294.4 5.8 cholesky.160
  308.6 5.8 cholesky.171
  315.8 4.9 custom-call.33
  323.5 23.1 %collective-permute-done.2 = bf16[64,8192]{1,0:T(8,128)(2,1)S(1)} collective-permute-done((bf16[64,8192]{1,0:T(8,128)(2,1)S(1)}, bf16[64,8192]{1,0:T(8,128)(2,1)S(1)}, u32[]{:S(2)}, u32[]{:S(2)}) %collective-permute-start.2) | collective-permute-done | bytes 1048608 | tf_op jit(solution)/shard_map/ppermute | solution.py:34
  354.2 163.1 %all-reduce.6.cloned.1.call-done = f32[128,128]{1,0:T(8,128)} async-done(((f32[128,128]{1,0:T(8,128)}), f32[128,128]{1,0:T(8,128)}) %all-reduce.6.cloned.1.call-update) | async-done | bytes 65552 | tf_op jit(solution)/shard_map/psum | solution.py:69
  520.9 5.8 cholesky.182
  528.1 4.9 custom-call.34
  536.8 5.8 cholesky.193
  551.0 5.8 cholesky.204
  558.2 4.9 custom-call.36
  570.6 20.7 %collective-permute-done.3 = bf16[64,8192]{1,0:T(8,128)(2,1)S(1)} collective-permute-done((bf16[64,8192]{1,0:T(8,128)(2,1)S(1)}, bf16[64,8192]{1,0:T(8,128)(2,1)S(1)}, u32[]{:S(2)}, u32[]{:S(2)}) %collective-permute-start.3) | collective-permute-done | bytes 1048608 | tf_op jit(solution)/shard_map/ppermute | solution.py:34
  592.9 21.1 %collective-permute-done.5 = bf16[64,8192]{1,0:T(8,128)(2,1)} collective-permute-done((bf16[64,8192]{1,0:T(8,128)(2,1)S(1)}, bf16[64,8192]{1,0:T(8,128)(2,1)}, u32[]{:S(2)}, u32[]{:S(2)}) %collective-permute-start.5) | collective-permute-done | bytes 1048608 | tf_op jit(solution)/shard_map/ppermute | solution.py:34
  616.6 145.8 %all-reduce.8.cloned.1.call-done = f32[128,128]{1,0:T(8,128)} async-done(((f32[128,128]{1,0:T(8,128)}), f32[128,128]{1,0:T(8,128)}) %all-reduce.8.cloned.1.call-update) | async-done | bytes 65552 | tf_op jit(solution)/shard_map/psum | solution.py:69
  766.0 5.8 cholesky.215
  781.8 5.8 cholesky.226
  789.0 4.9 custom-call.38
  796.0 5.8 cholesky.237
  (189 shorter events, 97.7 us)
Async XLA Ops:
  7.2 2.2 copy-start.5
  7.2 267.8 %all-reduce.4.cloned.1.call-start = ((), (), s32[]{:S(2)}) async-start(), calls=%async_computation | async-start | bytes 131072 | tf_op jit(solution)/shard_map/psum | solution.py:69
  9.3 3.2 copy-start
  11.4 7.7 copy-start.11
  12.5 27.9 %collective-permute-start = (bf16[128,512]{0,1:T(8,128)(2,1)S(1)}, bf16[128,512]{0,1:T(8,128)(2,1)S(1)}, u32[]{:S(2)}, u32[]{:S(2)}) collective-permute-start(bf16[128,512]{0,1:T(8,128)(2,1)S(1)} %get-tuple-element.6), channel_id=1, source_target_pairs={{0,4},{4,8},{8,12},{12,16},{16,20},{20,24},{24,28},{28,32},{32,36}... | collective-permute-start | bytes 393224 | tf_op jit(solution)/shard_map/ppermute | solution.py:19
  17.1 23.3 %collective-permute-start.1 = (bf16[128,512]{0,1:T(8,128)(2,1)S(1)}, bf16[128,512]{0,1:T(8,128)(2,1)S(1)}, u32[]{:S(2)}, u32[]{:S(2)}) collective-permute-start(bf16[128,512]{0,1:T(8,128)(2,1)S(1)} %get-tuple-element.7), channel_id=1, source_target_pairs={{4,0},{8,4},{12,8},{16,12},{20,16},{24,20},{28,24},{32,28},{36,32}... | collective-permute-start | bytes 393224 | tf_op jit(solution)/shard_map/ppermute | solution.py:22
  100.3 417.0 %all-reduce.6.cloned.1.call-start = ((), (), s32[]{:S(2)}) async-start(), calls=%async_computation.1 | async-start | bytes 131072 | tf_op jit(solution)/shard_map/psum | solution.py:69
  275.0 31.8 %copy-start.4 = (f32[128,128]{1,0:T(8,128)S(1)}, f32[128,128]{1,0:T(8,128)}, u32[]{:S(2)}) copy-start(f32[128,128]{1,0:T(8,128)} %all-reduce.4.cloned.1.call-done) | copy-start | bytes 196612
  322.2 24.4 %collective-permute-start.2 = (bf16[64,8192]{1,0:T(8,128)(2,1)S(1)}, bf16[64,8192]{1,0:T(8,128)(2,1)S(1)}, u32[]{:S(2)}, u32[]{:S(2)}) collective-permute-start(bf16[64,8192]{1,0:T(8,128)(2,1)S(1)} %convolution_convert_fusion.3), channel_id=1, source_target_pairs={{0,1},{1,0},{2,3},{3,2},{4,5},{5,4},{6,7},{7,6},{8,9},{9,8},{10,11... | collective-permute-start | bytes 3145736 | tf_op jit(solution)/shard_map/ppermute | solution.py:34
  346.8 1.0 copy-start.6
  346.8 1.4 copy-start.8
  346.8 2.8 copy-start.1
  349.5 412.9 %all-reduce.8.cloned.1.call-start = ((), (), s32[]{:S(2)}) async-start(), calls=%async_computation.2 | async-start | bytes 131072 | tf_op jit(solution)/shard_map/psum | solution.py:69
  352.5 211.2 %copy-start.7 = (bf16[64,8192]{1,0:T(8,128)(2,1)S(1)}, bf16[64,8192]{1,0:T(8,128)(2,1)}, u32[]{:S(2)}) copy-start(bf16[64,8192]{1,0:T(8,128)(2,1)} %copy-done.6) | copy-start | bytes 3145732
  352.5 215.7 %collective-permute-start.4 = (bf16[64,8192]{1,0:T(8,128)(2,1)S(1)}, bf16[64,8192]{1,0:T(8,128)(2,1)}, u32[]{:S(2)}, u32[]{:S(2)}) collective-permute-start(bf16[64,8192]{1,0:T(8,128)(2,1)S(1)} %convolution_convert_fusion.1), channel_id=1, source_target_pairs={{0,1},{1,0},{2,3},{3,2},{4,5},{5,4},{6,7},{7,6},{8,9},{9,8},{10,11... | collective-permute-start | bytes 3145736 | tf_op jit(solution)/shard_map/ppermute | solution.py:34
  517.4 31.8 %copy-start.2 = (f32[128,128]{1,0:T(8,128)S(1)}, f32[128,128]{1,0:T(8,128)}, u32[]{:S(2)}) copy-start(f32[128,128]{1,0:T(8,128)} %all-reduce.6.cloned.1.call-done) | copy-start | bytes 196612
  565.4 25.9 %collective-permute-start.3 = (bf16[64,8192]{1,0:T(8,128)(2,1)S(1)}, bf16[64,8192]{1,0:T(8,128)(2,1)S(1)}, u32[]{:S(2)}, u32[]{:S(2)}) collective-permute-start(bf16[64,8192]{1,0:T(8,128)(2,1)S(1)} %convolution_convert_fusion.2), channel_id=1, source_target_pairs={{0,2},{2,0},{1,3},{3,1},{4,6},{6,4},{5,7},{7,5},{8,10},{10,8},{9,1... | collective-permute-start | bytes 3145736 | tf_op jit(solution)/shard_map/ppermute | solution.py:34
  570.1 22.8 %copy-start.10 = (bf16[64,8192]{1,0:T(8,128)(2,1)}, bf16[64,8192]{1,0:T(8,128)(2,1)S(1)}, u32[]{:S(2)}) copy-start(bf16[64,8192]{1,0:T(8,128)(2,1)S(1)} %convolution_convert_fusion) | copy-start | bytes 3145732
  570.1 43.8 %collective-permute-start.5 = (bf16[64,8192]{1,0:T(8,128)(2,1)S(1)}, bf16[64,8192]{1,0:T(8,128)(2,1)}, u32[]{:S(2)}, u32[]{:S(2)}) collective-permute-start(bf16[64,8192]{1,0:T(8,128)(2,1)S(1)} %convolution_convert_fusion), channel_id=1, source_target_pairs={{0,2},{2,0},{1,3},{3,1},{4,6},{6,4},{5,7},{7,5},{8,10},{10,8},{9,1... | collective-permute-start | bytes 3145736 | tf_op jit(solution)/shard_map/ppermute | solution.py:34
  762.4 31.8 %copy-start.3 = (f32[128,128]{1,0:T(8,128)S(1)}, f32[128,128]{1,0:T(8,128)}, u32[]{:S(2)}) copy-start(f32[128,128]{1,0:T(8,128)} %all-reduce.8.cloned.1.call-done) | copy-start | bytes 196612
  808.1 1.2 copy-start.9
Sparse Core Ops, SparseCore 0:
  100.5 174.4 all-reduce.3
  349.6 167.6 all-reduce.5
  593.0 169.3 all-reduce.7
where the time goes:
time: 826 us; the launch traced here: 817 us
  waiting for transfers between devices  549 us (66%)
  other arithmetic  122 us (15%)
  matrix products  59.5 us (7%)
  local copies, waits for them, and re-layouts  59.3 us (7%)
  between operations  14.8 us (2%)
  starting transfers between devices  12.9 us (2%)
    psum x3, waiting for transfers between devices, coefficients_of(): return compress(lax.psum(local_gram, 'space'))  484 us
    ppermute x4, waiting for transfers between devices, partner(): return lax.ppermute(block, axis, route)  64.9 us
    another operation x27, other arithmetic, compress(): jnp.linalg.cholesky(inner_gram / (scales[:, None] * scales[None, :]))  58.7 us
    another operation x18, other arithmetic, compress(): lax.linalg.triangular_solve(factor_lower, normed, left_side=False, lower=...  49.9 us
    dot_general x1, matrix products, weigh_rows(): jnp.einsum('cbkq,kqbr->cbr', picked, factor, preferred_element_type=jnp.f...  29 us
    gather x1, local copies, waits for them, and re-layouts, weigh_rows(): picked = jnp.take(blocks, local_index, axis=1)  22.8 us
    reshape x1, local copies, waits for them, and re-layouts, weigh_rows(): factor = mass_factor.reshape(NEIGHBOURS, BLOCK_DOFS, -1, BLOCK_DOFS)  20.9 us
  transfers between devices with their start and end apart: 9, of which 6 were waited for; matrix products, arithmetic and copies ran while one was open for 10% of the time, Pallas kernels for 0%

commit v1 on v0

--- a/solution.py
+++ b/solution.py
@@ -66,7 +66,7 @@
 
 def coefficients_of(weighted):
     local_gram = jnp.dot(weighted, weighted.T, preferred_element_type=jnp.float32)
-    return compress(lax.psum(local_gram, "space"))
+    return compress(jnp.sum(lax.all_gather(local_gram, "space"), axis=0))
 
 
 def apply_coefficients(coefficients, stacked, weighted):

time: 826 us -> 549 us (0.66)
  waiting for transfers between devices: 549 us -> 274 us
  matrix products: 59.5 us -> 49.5 us
    psum x3 -> x0, waiting for transfers between devices: 484 us -> none  [coefficients_of(): return compress(lax.psum(local_gram, 'space'))]
    all_gather x0 -> x3, waiting for transfers between devices: none -> 184 us  [coefficients_of(): return compress(jnp.sum(lax.all_gather(local_gram, 'space'), axis=0))]
    ppermute x4, waiting for transfers between devices: 64.9 us -> 90.7 us  [partner(): return lax.ppermute(block, axis, route)]
  transfers between devices with their start and end apart: 9 -> 9, of which waited for: 6 -> 7; matrix products, arithmetic and copies ran while one was open for 10% -> 5% of each run, Pallas kernels for 0% -> 0%
where the time goes in v1:
time: 549 us; the launch traced here: 541 us
  waiting for transfers between devices  274 us (50%)
  other arithmetic  128 us (23%)
  local copies, waits for them, and re-layouts  58.8 us (11%)
  matrix products  49.5 us (9%)
  starting transfers between devices  15.3 us (3%)
  between operations  14.7 us (3%)
    all_gather x3, waiting for transfers between devices, coefficients_of(): return compress(jnp.sum(lax.all_gather(local_gram, 'space'), axis=0))  184 us
    ppermute x4, waiting for transfers between devices, partner(): return lax.ppermute(block, axis, route)  90.7 us
    another operation x27, other arithmetic, compress(): jnp.linalg.cholesky(inner_gram / (scales[:, None] * scales[None, :]))  58.7 us
    another operation x18, other arithmetic, compress(): lax.linalg.triangular_solve(factor_lower, normed, left_side=False, lower=...  49.9 us
    dot_general x1, matrix products, weigh_rows(): jnp.einsum('cbkq,kqbr->cbr', picked, factor, preferred_element_type=jnp.f...  29 us
    gather x1, local copies, waits for them, and re-layouts, weigh_rows(): picked = jnp.take(blocks, local_index, axis=1)  22.8 us
    reshape x1, local copies, waits for them, and re-layouts, weigh_rows(): factor = mass_factor.reshape(NEIGHBOURS, BLOCK_DOFS, -1, BLOCK_DOFS)  20.9 us
  transfers between devices with their start and end apart: 9, of which 7 were waited for; matrix products, arithmetic and copies ran while one was open for 5% of the time, Pallas kernels for 0%

profile of v1, /device:TPU:1, one launch (start us, length us, event | category | flops | bytes accessed | tf_op | source)
XLA Modules:
  0.0 541.3 jit_solution(17736405803509556532)
XLA Ops:
  19.5 20.9 %reshape.97 = bf16[7,64,128,64]{3,2,1,0:T(8,128)(2,1)} reshape(bf16[7,64,8192]{2,1,0:T(8,128)(2,1)} %param.9) | data formatting | bytes 14680064 | tf_op jit(solution)/shard_map/reshape | solution.py:42
  40.5 6.7 %pad_maximum_fusion = bf16[128,9216]{0,1:T(8,128)(2,1)S(1)} fusion(bf16[128,512]{0,1:T(8,128)(2,1)S(1)} %collective-permute-done.1, bf16[64,8192]{0,1:T(8,128)(2,1)} %copy.31, bf16[64,8192]{0,1:T(8,128)(2,1)} %copy-done, bf16[128,512]{0,1:T(8,128)(2,1)S(1)} %collective-permute-done), kind=kLoop, calls=%fused_computation.21 | loop fusion | flops 9437184 | bytes 4718592 | tf_op jit(solution)/shard_map/concatenate | solution.py:23
  47.1 22.8 %gather_fusion = bf16[896,128,64]{1,2,0:T(8,128)(2,1)} fusion(bf16[128,144,64]{0,2,1:T(8,128)(2,1)S(1)} %bitcast.181, s32[1024]{0:T(1024)S(1)} %pad_clamp_fusion), kind=kCustom, calls=%fused_computation | custom fusion | bytes 29363712 | tf_op jit(solution)/shard_map/jit(_take)/gather | solution.py:41
  69.9 29.0 %bitcast_convert_fusion = bf16[128,128,64]{1,2,0:T(8,128)(2,1)S(1)} fusion(bf16[128,7,128,64]{2,3,1,0:T(8,128)(2,1)} %bitcast.182, pred[128,7]{1,0:T(8,128)(4,1)S(1)} %copy.29, bf16[7,64,128,64]{3,2,1,0:T(8,128)(2,1)} %reshape.97), kind=kOutput, calls=%fused_computation.20 | convolution fusion | flops 947912704 | bytes 24118144 | tf_op jit(solution)/shard_map/cbkq,kqbr->cbr/dot_general | solution.py:43
  100.4 83.2 %all-gather.7.cloned.1.call-done = f32[8192,128]{1,0:T(8,128)} async-done(((f32[128,128]{1,0:T(8,128)}), f32[8192,128]{1,0:T(8,128)}) %all-gather.7.cloned.1.call-update) | async-done | bytes 4194320 | tf_op jit(solution)/shard_map/all_gather | solution.py:69
  187.9 5.8 %cholesky.149 = f32[64,64]{1,0:T(8,128)S(1)} custom-call(f32[64,64]{1,0:T(8,128)S(1)} %fusion.60), custom_call_target="Cholesky" | custom-call | tf_op jit(solution)/shard_map/jit(cholesky)/cholesky | solution.py:57
  202.0 5.8 %cholesky.160 = f32[64,64]{1,0:T(8,128)S(1)} custom-call(f32[64,64]{1,0:T(8,128)S(1)} %fusion.58), custom_call_target="Cholesky" | custom-call | tf_op jit(solution)/shard_map/jit(cholesky)/cholesky | solution.py:57
  209.2 4.9 custom-call.32
  216.2 5.8 %cholesky.171 = f32[64,64]{1,0:T(8,128)S(1)} custom-call(f32[64,64]{1,0:T(8,128)S(1)} %fusion.56), custom_call_target="Cholesky" | custom-call | tf_op jit(solution)/shard_map/jit(cholesky)/cholesky | solution.py:57
  231.1 23.4 %collective-permute-done.2 = bf16[64,8192]{1,0:T(8,128)(2,1)} collective-permute-done((bf16[64,8192]{1,0:T(8,128)(2,1)S(1)}, bf16[64,8192]{1,0:T(8,128)(2,1)}, u32[]{:S(2)}, u32[]{:S(2)}) %collective-permute-start.2) | collective-permute-done | bytes 1048608 | tf_op jit(solution)/shard_map/ppermute | solution.py:34
  257.7 76.7 %all-gather.9.cloned.1.call-done = f32[8192,128]{1,0:T(8,128)} async-done(((f32[128,128]{1,0:T(8,128)}), f32[8192,128]{1,0:T(8,128)}) %all-gather.9.cloned.1.call-update) | async-done | bytes 4194320 | tf_op jit(solution)/shard_map/all_gather | solution.py:69
  338.6 5.8 %cholesky.182 = f32[64,64]{1,0:T(8,128)S(1)} custom-call(f32[64,64]{1,0:T(8,128)S(1)} %fusion.54), custom_call_target="Cholesky" | custom-call | tf_op jit(solution)/shard_map/jit(cholesky)/cholesky | solution.py:57
  352.8 5.8 %cholesky.193 = f32[64,64]{1,0:T(8,128)S(1)} custom-call(f32[64,64]{1,0:T(8,128)S(1)} %fusion.52), custom_call_target="Cholesky" | custom-call | tf_op jit(solution)/shard_map/jit(cholesky)/cholesky | solution.py:57
  360.0 4.9 custom-call.35
  367.0 5.8 %cholesky.204 = f32[64,64]{1,0:T(8,128)S(1)} custom-call(f32[64,64]{1,0:T(8,128)S(1)} %fusion.50), custom_call_target="Cholesky" | custom-call | tf_op jit(solution)/shard_map/jit(cholesky)/cholesky | solution.py:57
  383.0 23.2 %collective-permute-done.3 = bf16[64,8192]{1,0:T(8,128)(2,1)S(1)} collective-permute-done((bf16[64,8192]{1,0:T(8,128)(2,1)S(1)}, bf16[64,8192]{1,0:T(8,128)(2,1)S(1)}, u32[]{:S(2)}, u32[]{:S(2)}) %collective-permute-start.3) | collective-permute-done | bytes 1048608 | tf_op jit(solution)/shard_map/ppermute | solution.py:34
  413.1 22.5 %collective-permute-done.4 = bf16[64,8192]{1,0:T(8,128)(2,1)S(1)} collective-permute-done((bf16[64,8192]{1,0:T(8,128)(2,1)S(1)}, bf16[64,8192]{1,0:T(8,128)(2,1)S(1)}, u32[]{:S(2)}, u32[]{:S(2)}) %collective-permute-start.4) | collective-permute-done | bytes 1048608 | tf_op jit(solution)/shard_map/ppermute | solution.py:34
  439.1 21.6 %collective-permute-done.5 = bf16[64,8192]{1,0:T(8,128)(2,1)S(1)} collective-permute-done((bf16[64,8192]{1,0:T(8,128)(2,1)S(1)}, bf16[64,8192]{1,0:T(8,128)(2,1)S(1)}, u32[]{:S(2)}, u32[]{:S(2)}) %collective-permute-start.5) | collective-permute-done | bytes 1048608 | tf_op jit(solution)/shard_map/ppermute | solution.py:34
  462.2 23.7 %all-gather.11.cloned.1.call-done = f32[8192,128]{1,0:T(8,128)} async-done(((f32[128,128]{1,0:T(8,128)}), f32[8192,128]{1,0:T(8,128)}) %all-gather.11.cloned.1.call-update) | async-done | bytes 4194320 | tf_op jit(solution)/shard_map/all_gather | solution.py:69
  490.1 5.8 %cholesky.215 = f32[64,64]{1,0:T(8,128)S(1)} custom-call(f32[64,64]{1,0:T(8,128)S(1)} %fusion.48), custom_call_target="Cholesky" | custom-call | tf_op jit(solution)/shard_map/jit(cholesky)/cholesky | solution.py:57
  497.3 4.9 custom-call.37
  504.3 5.8 %cholesky.226 = f32[64,64]{1,0:T(8,128)S(1)} custom-call(f32[64,64]{1,0:T(8,128)S(1)} %fusion.46), custom_call_target="Cholesky" | custom-call | tf_op jit(solution)/shard_map/jit(cholesky)/cholesky | solution.py:57
  518.5 5.8 %cholesky.237 = f32[64,64]{1,0:T(8,128)S(1)} custom-call(f32[64,64]{1,0:T(8,128)S(1)} %fusion.44), custom_call_target="Cholesky" | custom-call | tf_op jit(solution)/shard_map/jit(cholesky)/cholesky | solution.py:57
  525.7 4.9 custom-call.39
  (180 shorter events, 100.6 us)
Async XLA Ops:
  7.2 2.2 copy-start.2
  7.2 176.5 %all-gather.7.cloned.1.call-start = ((), (), s32[]{:S(2)}) async-start(), calls=%async_computation | async-start | bytes 4259840 | tf_op jit(solution)/shard_map/all_gather | solution.py:69
  9.3 3.2 copy-start
  11.4 7.7 %copy-start.5 = (s32[128,7]{0,1:T(8,128)S(1)}, s32[128,7]{0,1:T(8,128)}, u32[]{:S(2)}) copy-start(s32[128,7]{0,1:T(8,128)} %param.10) | copy-start | bytes 10756
  12.5 27.9 %collective-permute-start = (bf16[128,512]{0,1:T(8,128)(2,1)S(1)}, bf16[128,512]{0,1:T(8,128)(2,1)S(1)}, u32[]{:S(2)}, u32[]{:S(2)}) collective-permute-start(bf16[128,512]{0,1:T(8,128)(2,1)S(1)} %get-tuple-element.6), channel_id=1, source_target_pairs={{0,4},{4,8},{8,12},{12,16},{16,20},{20,24},{24,28},{28,32},{32,36}... | collective-permute-start | bytes 393224 | tf_op jit(solution)/shard_map/ppermute | solution.py:19
  17.1 23.3 %collective-permute-start.1 = (bf16[128,512]{0,1:T(8,128)(2,1)S(1)}, bf16[128,512]{0,1:T(8,128)(2,1)S(1)}, u32[]{:S(2)}, u32[]{:S(2)}) collective-permute-start(bf16[128,512]{0,1:T(8,128)(2,1)S(1)} %get-tuple-element.7), channel_id=1, source_target_pairs={{4,0},{8,4},{12,8},{16,12},{20,16},{24,20},{28,24},{32,28},{36,32}... | collective-permute-start | bytes 393224 | tf_op jit(solution)/shard_map/ppermute | solution.py:22
  100.3 234.1 %all-gather.9.cloned.1.call-start = ((), (), s32[]{:S(2)}) async-start(), calls=%async_computation.1 | async-start | bytes 4259840 | tf_op jit(solution)/shard_map/all_gather | solution.py:69
  229.9 24.6 %collective-permute-start.2 = (bf16[64,8192]{1,0:T(8,128)(2,1)S(1)}, bf16[64,8192]{1,0:T(8,128)(2,1)}, u32[]{:S(2)}, u32[]{:S(2)}) collective-permute-start(bf16[64,8192]{1,0:T(8,128)(2,1)S(1)} %convolution_convert_fusion.3), channel_id=1, source_target_pairs={{0,1},{1,0},{2,3},{3,2},{4,5},{5,4},{6,7},{7,6},{8,9},{9,8},{10,11... | collective-permute-start | bytes 3145736 | tf_op jit(solution)/shard_map/ppermute | solution.py:34
  257.2 228.7 %all-gather.11.cloned.1.call-start = ((), (), s32[]{:S(2)}) async-start(), calls=%async_computation.2 | async-start | bytes 4259840 | tf_op jit(solution)/shard_map/all_gather | solution.py:69
  380.2 26.0 %collective-permute-start.3 = (bf16[64,8192]{1,0:T(8,128)(2,1)S(1)}, bf16[64,8192]{1,0:T(8,128)(2,1)S(1)}, u32[]{:S(2)}, u32[]{:S(2)}) collective-permute-start(bf16[64,8192]{1,0:T(8,128)(2,1)S(1)} %convolution_convert_fusion.2), channel_id=1, source_target_pairs={{0,2},{2,0},{1,3},{3,1},{4,6},{6,4},{5,7},{7,5},{8,10},{10,8},{9,1... | collective-permute-start | bytes 3145736 | tf_op jit(solution)/shard_map/ppermute | solution.py:34
  406.4 1.0 copy-start.3
  406.4 2.3 copy-start.1
  411.7 23.9 %collective-permute-start.4 = (bf16[64,8192]{1,0:T(8,128)(2,1)S(1)}, bf16[64,8192]{1,0:T(8,128)(2,1)S(1)}, u32[]{:S(2)}, u32[]{:S(2)}) collective-permute-start(bf16[64,8192]{1,0:T(8,128)(2,1)S(1)} %convolution_convert_fusion.1), channel_id=1, source_target_pairs={{0,1},{1,0},{2,3},{3,2},{4,5},{5,4},{6,7},{7,6},{8,9},{9,8},{10,11... | collective-permute-start | bytes 3145736 | tf_op jit(solution)/shard_map/ppermute | solution.py:34
  436.3 24.4 %collective-permute-start.5 = (bf16[64,8192]{1,0:T(8,128)(2,1)S(1)}, bf16[64,8192]{1,0:T(8,128)(2,1)S(1)}, u32[]{:S(2)}, u32[]{:S(2)}) collective-permute-start(bf16[64,8192]{1,0:T(8,128)(2,1)S(1)} %convolution_convert_fusion), channel_id=1, source_target_pairs={{0,2},{2,0},{1,3},{3,1},{4,6},{6,4},{5,7},{7,5},{8,10},{10,8},{9,1... | collective-permute-start | bytes 3145736 | tf_op jit(solution)/shard_map/ppermute | solution.py:34
  488.3 42.9 %copy-start.4 = (bf16[64,8192]{1,0:T(8,128)(2,1)S(1)}, bf16[64,8192]{1,0:T(8,128)(2,1)}, u32[]{:S(2)}) copy-start(bf16[64,8192]{1,0:T(8,128)(2,1)} %copy-done.3) | copy-start | bytes 3145732
Sparse Core Ops, SparseCore 0:
  100.5 83.1 all-gather.6
  257.3 77.0 all-gather.8
  408.8 77.0 all-gather.10
